TPU v7x, 32 devices: a whole 2x2x4 slice. The times are simulated.
32 devices in a mesh: fsdp: 4 (over y, x), seq: 8 (over z, core).
Axes of the slice: x: 2, y: 2, z: 4, core: 2. Of those that a mesh axis runs over, the one named last changes fastest.
Arguments:
- residual_in: bfloat16 [4, 1024, 2048], P('fsdp', 'seq'), may hold values from -6 to 6
- attn_gain: bfloat16 [2048], replicated, may hold values from 0.5 to 1.5
- mlp_gain: bfloat16 [2048], replicated, may hold values from 0.5 to 1.5
- w_qkv: bfloat16 [2048, 3, 2048], P('fsdp'), may hold values from -0.125 to 0.125
- w_out: bfloat16 [2048, 2048], P('fsdp'), may hold values from -1 to 1
- w_gate_up: bfloat16 [8192, 2, 2048], P('fsdp'), may hold values from -0.125 to 0.125
- w_down: bfloat16 [2048, 8192], P('fsdp'), may hold values from -0.0625 to 0.0625
- cotangent: bfloat16 [4, 1024, 2048], P('fsdp', 'seq'), may hold values from -6 to 6
Outputs:
- layer_out: bfloat16 [4, 1024, 2048], P('fsdp', 'seq')
- grad_input: float32 [4, 1024, 2048], P('fsdp', 'seq')
- grad_attn_gain: float32 [2048], P(('fsdp', 'seq'))
- grad_mlp_gain: float32 [2048], P(('fsdp', 'seq'))
- grad_qkv: float32 [2048, 3, 2048], P(('seq', 'fsdp'))
- grad_out_proj: float32 [2048, 2048], P(None, ('seq', 'fsdp'))
- grad_gate_up: float32 [8192, 2, 2048], P(('seq', 'fsdp'))
- grad_down: float32 [2048, 8192], P(None, ('seq', 'fsdp'))
All inputs are finite; a program needn't handle non-finite values.
Results may differ from a plain program's by a relative error of at most 0.018.
Values may be sent and summed in bfloat16 or wider, within the bound.
No kernel may reach another device: no remote copies, remote signals or barrier semaphores. Data moves between devices by JAX's collectives and lax.ppermute only.
A program may use at most 384 MiB of HBM per device.

v0:
```python
import math
import jax
import jax.numpy as jnp
from jax import lax
from jax.sharding import PartitionSpec as P

HD = 64
NORM_EPS = 1e-05
ROPE_BASE = 130000.0


def rotate(matrix):
    shaped = matrix.reshape(matrix.shape[:-1] + (matrix.shape[-1] // HD, 2, HD // 2))
    turned = jnp.stack([-shaped[..., 1, :], shaped[..., 0, :]], axis=-2)
    return turned.reshape(matrix.shape)


def rotate_back(matrix):
    shaped = matrix.reshape(matrix.shape[:-1] + (matrix.shape[-1] // HD, 2, HD // 2))
    turned = jnp.stack([shaped[..., 1, :], -shaped[..., 0, :]], axis=-2)
    return turned.reshape(matrix.shape)


def rope_tables(positions, columns):
    freq_index = (jnp.arange(columns, dtype=jnp.int32) % (HD // 2)).astype(jnp.float32)
    inverse = ROPE_BASE ** (-2.0 * freq_index / HD)
    angles = positions.astype(jnp.float32)[:, None] * inverse[None, :]
    return (jnp.cos(angles), jnp.sin(angles))


def rms_scale(matrix):
    return lax.rsqrt(jnp.mean(matrix * matrix, axis=-1, keepdims=True) + NORM_EPS)


def rms_back(grad_normed, matrix, scale_rows, gain):
    weighted = grad_normed * gain
    inner_mean = jnp.mean(weighted * matrix, axis=-1, keepdims=True)
    grad_matrix = scale_rows * weighted - matrix * scale_rows**3 * inner_mean
    grad_gain = jnp.sum(grad_normed * matrix * scale_rows, axis=0)
    return (grad_matrix, grad_gain)


def attend_forward(queries, key_rows, values):
    seq_count, length, width_here = queries.shape
    heads_here = width_here // HD
    q_block = min(512, length)
    k_block = min(256, length)
    inv_root = 1.0 / math.sqrt(HD)
    shaped_q = queries.reshape(seq_count, length, heads_here, HD)
    shaped_k = key_rows.reshape(seq_count, length, heads_here, HD)
    shaped_v = values.reshape(seq_count, length, heads_here, HD)

    def query_step(q_index, carried):
        attended, totals = carried
        offset = q_index * q_block
        q_rows = lax.dynamic_slice_in_dim(shaped_q, offset, q_block, 1)
        query_pos = offset + jnp.arange(q_block, dtype=jnp.int32)

        def key_step(k_index, running):
            unnorm, denominator = running
            k_start = k_index * k_block
            k_rows = lax.dynamic_slice_in_dim(shaped_k, k_start, k_block, 1)
            v_rows = lax.dynamic_slice_in_dim(shaped_v, k_start, k_block, 1)
            scores = (
                jnp.einsum("bqhd,bkhd->bhqk", q_rows, k_rows, preferred_element_type=jnp.float32)
                * inv_root
            )
            causal = (k_start + jnp.arange(k_block, dtype=jnp.int32))[None, :] <= query_pos[:, None]
            exp_scores = jnp.where(causal, jnp.exp(scores), 0.0)
            denominator = denominator + jnp.sum(exp_scores, axis=-1)
            unnorm = unnorm + jnp.einsum(
                "bhqk,bkhd->bqhd",
                exp_scores.astype(jnp.bfloat16),
                v_rows,
                preferred_element_type=jnp.float32,
            )
            return (unnorm, denominator)

        start_state = (
            jnp.zeros((seq_count, q_block, heads_here, HD), jnp.float32),
            jnp.zeros((seq_count, heads_here, q_block), jnp.float32),
        )
        unnorm, denominator = lax.fori_loop(0, (offset + q_block) // k_block, key_step, start_state)
        block_out = unnorm / jnp.transpose(denominator, (0, 2, 1))[..., None]
        attended = lax.dynamic_update_slice_in_dim(attended, block_out, offset, 1)
        totals = lax.dynamic_update_slice_in_dim(totals, denominator, offset, 2)
        return (attended, totals)

    initial = (
        jnp.zeros((seq_count, length, heads_here, HD), jnp.float32),
        jnp.zeros((seq_count, heads_here, length), jnp.float32),
    )
    attended, totals = lax.fori_loop(0, length // q_block, query_step, initial)
    return (attended.reshape(seq_count, length, width_here), totals)


def attend_backward(queries, key_rows, values, attended, totals, grad_attended):
    seq_count, length, width_here = queries.shape
    heads_here = width_here // HD
    q_block = min(512, length)
    k_block = min(256, length)
    inv_root = 1.0 / math.sqrt(HD)
    shaped_q = queries.reshape(seq_count, length, heads_here, HD)
    shaped_k = key_rows.reshape(seq_count, length, heads_here, HD)
    shaped_v = values.reshape(seq_count, length, heads_here, HD)
    shaped_grad = grad_attended.reshape(seq_count, length, heads_here, HD).astype(jnp.float32)
    shaped_att = attended.reshape(seq_count, length, heads_here, HD)
    totals_rows = jnp.transpose(totals, (0, 2, 1))
    grad_total = -jnp.sum(shaped_grad * shaped_att, axis=-1) / totals_rows
    grad_unnorm = (shaped_grad / totals_rows[..., None]).astype(jnp.bfloat16)

    def query_step(q_index, carried):
        grad_q, grad_k, grad_v = carried
        offset = q_index * q_block
        q_rows = lax.dynamic_slice_in_dim(shaped_q, offset, q_block, 1)
        g_rows = lax.dynamic_slice_in_dim(grad_unnorm, offset, q_block, 1)
        total_rows = jnp.transpose(
            lax.dynamic_slice_in_dim(grad_total, offset, q_block, 1), (0, 2, 1)
        )
        query_pos = offset + jnp.arange(q_block, dtype=jnp.int32)

        def key_step(k_index, running):
            dq_acc, dk_all, dv_all = running
            k_start = k_index * k_block
            k_rows = lax.dynamic_slice_in_dim(shaped_k, k_start, k_block, 1)
            v_rows = lax.dynamic_slice_in_dim(shaped_v, k_start, k_block, 1)
            scores = (
                jnp.einsum("bqhd,bkhd->bhqk", q_rows, k_rows, preferred_element_type=jnp.float32)
                * inv_root
            )
            causal = (k_start + jnp.arange(k_block, dtype=jnp.int32))[None, :] <= query_pos[:, None]
            exp_scores = jnp.where(causal, jnp.exp(scores), 0.0)
            grad_prob = jnp.einsum(
                "bqhd,bkhd->bhqk", g_rows, v_rows, preferred_element_type=jnp.float32
            )
            grad_scores = (exp_scores * (grad_prob + total_rows[..., None])).astype(jnp.bfloat16)
            dq_acc = (
                dq_acc
                + jnp.einsum(
                    "bhqk,bkhd->bqhd", grad_scores, k_rows, preferred_element_type=jnp.float32
                )
                * inv_root
            )
            dk_part = (
                jnp.einsum(
                    "bhqk,bqhd->bkhd", grad_scores, q_rows, preferred_element_type=jnp.float32
                )
                * inv_root
            )
            dv_part = jnp.einsum(
                "bhqk,bqhd->bkhd",
                exp_scores.astype(jnp.bfloat16),
                g_rows,
                preferred_element_type=jnp.float32,
            )
            dk_slice = lax.dynamic_slice_in_dim(dk_all, k_start, k_block, 1) + dk_part
            dv_slice = lax.dynamic_slice_in_dim(dv_all, k_start, k_block, 1) + dv_part
            dk_all = lax.dynamic_update_slice_in_dim(dk_all, dk_slice, k_start, 1)
            dv_all = lax.dynamic_update_slice_in_dim(dv_all, dv_slice, k_start, 1)
            return (dq_acc, dk_all, dv_all)

        start_state = (jnp.zeros((seq_count, q_block, heads_here, HD), jnp.float32), grad_k, grad_v)
        dq_block, grad_k, grad_v = lax.fori_loop(
            0, (offset + q_block) // k_block, key_step, start_state
        )
        grad_q = lax.dynamic_update_slice_in_dim(grad_q, dq_block, offset, 1)
        return (grad_q, grad_k, grad_v)

    empty = jnp.zeros((seq_count, length, heads_here, HD), jnp.float32)
    grad_q, grad_k, grad_v = lax.fori_loop(0, length // q_block, query_step, (empty, empty, empty))
    cosine, sine_table = rope_tables(jnp.arange(length, dtype=jnp.int32), width_here)
    grad_q = grad_q.reshape(seq_count, length, width_here)
    grad_k = grad_k.reshape(seq_count, length, width_here)
    grad_v = grad_v.reshape(seq_count, length, width_here)
    raw_q = grad_q * cosine + rotate_back(grad_q * sine_table)
    raw_k = grad_k * cosine + rotate_back(grad_k * sine_table)
    return jnp.stack([raw_q, raw_k, grad_v]).astype(jnp.bfloat16)


def body(residual_in, attn_gain, mlp_gain, w_qkv, w_out, w_gate_up, w_down, cotangent):
    seq_count, shard_len, model_width = residual_in.shape
    tokens = seq_count * shard_len
    seq_index = lax.axis_index("seq")
    positions = seq_index * shard_len + jnp.arange(tokens, dtype=jnp.int32) % shard_len
    cosine, sine_table = rope_tables(positions, model_width)
    inputs = residual_in.reshape(tokens, model_width).astype(jnp.float32)
    gain_one = attn_gain.astype(jnp.float32)
    gain_two = mlp_gain.astype(jnp.float32)
    scale_one = rms_scale(inputs)
    normed_one = (inputs * scale_one * gain_one).astype(jnp.bfloat16)
    qkv_full, out_full = (
        lax.all_gather(w_qkv, "fsdp", axis=0, tiled=True),
        lax.all_gather(w_out, "fsdp", axis=0, tiled=True),
    )
    projected = jnp.einsum("td,fpd->ptf", normed_one, qkv_full, preferred_element_type=jnp.float32)
    queries = (projected[0] * cosine + rotate(projected[0]) * sine_table).astype(jnp.bfloat16)
    key_rows = (projected[1] * cosine + rotate(projected[1]) * sine_table).astype(jnp.bfloat16)
    values = projected[2].astype(jnp.bfloat16)
    stacked = jnp.stack([queries, key_rows, values]).reshape(3, seq_count, shard_len, model_width)
    head_view = lax.all_to_all(stacked, "seq", split_axis=3, concat_axis=2, tiled=True)
    attended, totals = attend_forward(head_view[0], head_view[1], head_view[2])
    attended_heads = attended.astype(jnp.bfloat16)
    sent_back = lax.all_to_all(attended_heads, "seq", split_axis=1, concat_axis=2, tiled=True)
    attended_low = sent_back.reshape(tokens, model_width)
    branch = jnp.einsum("ti,fi->tf", attended_low, out_full, preferred_element_type=jnp.float32)
    residual = inputs + branch
    scale_two = rms_scale(residual)
    normed_two = (residual * scale_two * gain_two).astype(jnp.bfloat16)
    up_full, down_full = (
        lax.all_gather(w_gate_up, "fsdp", axis=0, tiled=True),
        lax.all_gather(w_down, "fsdp", axis=0, tiled=True),
    )
    gate_up = jnp.einsum("td,jpd->ptj", normed_two, up_full, preferred_element_type=jnp.float32)
    hidden = (jax.nn.silu(gate_up[0]) * gate_up[1]).astype(jnp.bfloat16)
    mlp_term = jnp.einsum("tj,fj->tf", hidden, down_full, preferred_element_type=jnp.float32)
    layer_out = (
        (residual + mlp_term).astype(jnp.bfloat16).reshape(seq_count, shard_len, model_width)
    )
    grad_out = cotangent.reshape(tokens, model_width)
    up_again, down_again = (
        lax.all_gather(w_gate_up, "fsdp", axis=0, tiled=True),
        lax.all_gather(w_down, "fsdp", axis=0, tiled=True),
    )
    grad_hidden = jnp.einsum("tf,fj->tj", grad_out, down_again, preferred_element_type=jnp.float32)
    sigmoid_gate = jax.nn.sigmoid(gate_up[0])
    grad_gate = grad_hidden * gate_up[1] * sigmoid_gate * (1.0 + gate_up[0] * (1.0 - sigmoid_gate))
    grad_up = grad_hidden * jax.nn.silu(gate_up[0])
    grad_gu = jnp.stack([grad_gate, grad_up]).astype(jnp.bfloat16)
    grad_normed_two = jnp.einsum(
        "ptj,jpd->td", grad_gu, up_again, preferred_element_type=jnp.float32
    )
    ff_width = grad_gu.shape[2]
    unit_rows = jnp.concatenate([grad_gu, hidden[None]], axis=0).reshape(
        3, seq_count, shard_len, ff_width
    )
    unit_cols = lax.all_to_all(unit_rows, "seq", split_axis=3, concat_axis=2, tiled=True)
    normed_piece = lax.all_gather(
        normed_two.reshape(seq_count, shard_len, model_width), "seq", axis=1, tiled=True
    )
    grad_piece = lax.all_gather(cotangent, "seq", axis=1, tiled=True)
    gu_part = jnp.einsum(
        "psnj,snd->jpd", unit_cols[:2], normed_piece, preferred_element_type=jnp.float32
    )
    down_part = jnp.einsum(
        "snf,snj->fj", grad_piece, unit_cols[2], preferred_element_type=jnp.float32
    )
    gu_part, down_part = (gu_part, down_part)
    grad_gate_up, grad_down = (
        lax.psum_scatter(
            gu_part.astype(jnp.bfloat16), "fsdp", scatter_dimension=0, tiled=True
        ).astype(jnp.float32),
        lax.psum_scatter(
            down_part.astype(jnp.bfloat16), "fsdp", scatter_dimension=1, tiled=True
        ).astype(jnp.float32),
    )
    grad_norm_two, grad_gain_two = rms_back(grad_normed_two, residual, scale_two, gain_two)
    grad_residual = grad_out.astype(jnp.float32) + grad_norm_two
    qkv_back, out_back = (
        lax.all_gather(w_qkv, "fsdp", axis=0, tiled=True),
        lax.all_gather(w_out, "fsdp", axis=0, tiled=True),
    )
    grad_branch = grad_residual.astype(jnp.bfloat16)
    grad_attended = jnp.einsum(
        "tf,fi->ti", grad_branch, out_back, preferred_element_type=jnp.float32
    )
    grad_attended = grad_attended.astype(jnp.bfloat16).reshape(seq_count, shard_len, model_width)
    grad_heads = lax.all_to_all(grad_attended, "seq", split_axis=2, concat_axis=1, tiled=True)
    grad_stacked = attend_backward(
        head_view[0], head_view[1], head_view[2], attended, totals, grad_heads
    )
    normed_piece = lax.all_gather(
        normed_one.reshape(seq_count, shard_len, model_width), "seq", axis=1, tiled=True
    )
    branch_piece = lax.all_gather(
        grad_branch.reshape(seq_count, shard_len, model_width), "seq", axis=1, tiled=True
    )
    grad_piece = grad_stacked
    qkv_part = jnp.einsum(
        "psnf,snd->fpd", grad_piece, normed_piece, preferred_element_type=jnp.float32
    )
    out_part = jnp.einsum(
        "snf,sni->fi", branch_piece, attended_heads, preferred_element_type=jnp.float32
    )
    qkv_part, out_part = (qkv_part, out_part)
    grad_qkv, grad_out_proj = (
        lax.psum_scatter(
            qkv_part.astype(jnp.bfloat16), "fsdp", scatter_dimension=0, tiled=True
        ).astype(jnp.float32),
        lax.psum_scatter(
            out_part.astype(jnp.bfloat16), "fsdp", scatter_dimension=1, tiled=True
        ).astype(jnp.float32),
    )
    grad_projected = lax.all_to_all(grad_stacked, "seq", split_axis=2, concat_axis=3, tiled=True)
    grad_projected = grad_projected.reshape(3, tokens, model_width)
    grad_normed_one = jnp.einsum(
        "ptf,fpd->td", grad_projected, qkv_back, preferred_element_type=jnp.float32
    )
    grad_norm_one, grad_gain_one = rms_back(grad_normed_one, inputs, scale_one, gain_one)
    grad_input = (grad_residual + grad_norm_one).reshape(seq_count, shard_len, model_width)
    grad_attn_gain, grad_mlp_gain = (
        lax.psum_scatter(grad_gain_one, ("fsdp", "seq"), scatter_dimension=0, tiled=True),
        lax.psum_scatter(grad_gain_two, ("fsdp", "seq"), scatter_dimension=0, tiled=True),
    )
    return (
        layer_out,
        grad_input,
        grad_attn_gain,
        grad_mlp_gain,
        grad_qkv,
        grad_out_proj,
        grad_gate_up,
        grad_down,
    )


def solution(mesh):
    return jax.shard_map(
        body,
        mesh=mesh,
        in_specs=(
            P("fsdp", "seq", None),
            P(),
            P(),
            P("fsdp", None, None),
            P("fsdp", None),
            P("fsdp", None, None),
            P("fsdp", None),
            P("fsdp", "seq", None),
        ),
        out_specs=(
            P("fsdp", "seq", None),
            P("fsdp", "seq", None),
            P(("fsdp", "seq")),
            P(("fsdp", "seq")),
            P(("seq", "fsdp"), None, None),
            P(None, ("seq", "fsdp")),
            P(("seq", "fsdp"), None, None),
            P(None, ("seq", "fsdp")),
        ),
        check_vma=False,
    )
```

profile of v0, /device:TPU:0, one launch (start us, length us, event | category | flops | bytes accessed | tf_op | source)
XLA Modules:
  0.0 1827.8 jit_solution(5378411040820716253)
XLA Ops:
  8.7 18.1 copy.202
  28.7 211.5 %all-gather.11.cloned.1.call-done = bf16[2048,3,2048]{2,0,1:T(8,128)(2,1)} async-done(((bf16[512,3,2048]{2,0,1:T(8,128)(2,1)}), bf16[2048,3,2048]{2,0,1:T(8,128)(2,1)}) %all-gather.11.cloned.1.call-update) | async-done | bytes 25165840 | tf_op jit(solution)/shard_map/all_gather | solution.py:192
  240.2 13.5 convolution_bitcast_fusion.3
  284.0 49.0 %all-to-all-done = bf16[3,1,128,2048]{2,0,1,3:T(4,128)(2,1)S(1)} async-done(((bf16[3,1,128,2048]{2,0,1,3:T(4,128)(2,1)}), bf16[3,1,128,2048]{2,0,1,3:T(4,128)(2,1)S(1)}, u32[]{:S(2)}, u32[]{:S(2)}) %all-to-all-start) | async-done | bytes 1572896 | tf_op jit(solution)/shard_map/all_to_all | solution.py:200
  340.4 17.2 while.118
  347.3 10.2 while.121
  376.2 14.0 all-to-all-done.1
  402.0 506.1 %all-gather.15.cloned.1.call-done = bf16[8192,2,2048]{2,0,1:T(8,128)(2,1)} async-done(((bf16[2048,2,2048]{2,0,1:T(8,128)(2,1)}), bf16[8192,2,2048]{2,0,1:T(8,128)(2,1)}) %all-gather.15.cloned.1.call-update) | async-done | bytes 67108880 | tf_op jit(solution)/shard_map/all_gather | solution.py:210
  908.1 37.6 %convolution_bitcast_fusion.2 = f32[2,128,8192]{2,1,0:T(8,128)} fusion(bf16[8192,2,2048]{2,0,1:T(8,128)(2,1)} %all-gather.15.cloned.1.call-done, bf16[128,2048]{1,0:T(8,128)(2,1)S(1)} %multiply_convert_fusion.2), kind=kOutput, calls=%fused_computation.67 | convolution fusion | flops 8589934592 | bytes 76021760 | tf_op jit(solution)/shard_map/td,jpd->ptj/dot_general | solution.py:213
  945.7 261.2 %all-gather.17.cloned.1.call-done = bf16[2048,8192]{1,0:T(8,128)(2,1)} async-done(((bf16[512,8192]{1,0:T(8,128)(2,1)}), bf16[2048,8192]{1,0:T(8,128)(2,1)}) %all-gather.17.cloned.1.call-update) | async-done | bytes 33554448 | tf_op jit(solution)/shard_map/all_gather | solution.py:211
  1206.9 19.1 %fusion.83 = (bf16[1,128,8192]{2,1,0:T(8,128)(2,1)}, bf16[1,128,8192]{2,1,0:T(8,128)(2,1)}) fusion(f32[2,128,8192]{2,1,0:T(8,128)} %convolution_bitcast_fusion.2, bf16[2048,8192]{1,0:T(8,128)(2,1)} %all-gather.17.cloned.1.call-done, bf16[1,128,2048]{2,1,0:T(8,128)(2,1)} %param.23), kind=kOutput, calls=%fused_computation.108 | convolution fusion | flops 4308598784 | bytes 46661632 | tf_op jit(solution)/shard_map/tf,fj->tj/dot_general | solution.py:224
  1226.0 25.3 %multiply_reduce_fusion = (f32[2048]{0:T(1024)}, f32[128]{0:T(128)S(1)}, f32[128,2048]{1,0:T(8,128)S(1)}) fusion(f32[128,2048]{1,0:T(8,128)S(1)} %get-tuple-element.716, f32[128]{0:T(128)S(1)} %get-tuple-element.714, f32[2048]{0:T(1024)S(1)} %convert_element_type.212, bf16[8192,2,2048]{2,0,1:T(8,128)(2,1)} %all-gather.15.cloned.1.call-done, ...), kind=kOutput, calls=%fused_computation.151 | convolution fusion | flops 8593602560 | bytes 73417728 | tf_op jit(solution)/shard_map/ptj,jpd->td/dot_general | solution.py:229
  1266.0 11.5 reduce.4
  1289.4 13.2 copy.216
  1329.4 37.3 %while.120 = (s32[]{:T(128)}, f32[1,1024,4,64]{1,3,2,0:T(8,128)}, f32[1,1024,4,64]{1,3,2,0:T(8,128)S(1)}, f32[1,1024,4,64]{1,3,2,0:T(8,128)}, bf16[1,1024,4,64]{...) while((s32[]{:T(128)}, f32[1,1024,4,64]{1,3,2,0:T(8,128)}, ...), condition=%wide.region_12.13_spmd, body=%wide.region_9.12_spmd.sunk | while | flops 340329248 | bytes 17070880 | solution.py:170
  1331.2 10.7 while.122
  1344.5 21.4 %while.122 = (s32[]{:T(128)}, f32[1,512,4,64]{1,3,2,0:T(8,128)S(1)}, f32[1,1024,4,64]{1,3,2,0:T(8,128)S(1)}, f32[1,1024,4,64]{1,3,2,0:T(8,128)}, s32[]{:T(128)},...) while((s32[]{:T(128)}, f32[1,512,4,64]{1,3,2,0:T(8,128)S(1)}, ...), condition=%wide.region_11.11_spmd.clone, body=%wide.region_10.10_spmd.clone.sunk | while | flops 340329216 | bytes 14432507 | solution.py:163
  1410.0 157.5 %all-to-all-done.4 = bf16[3,1,128,8192]{2,0,1,3:T(4,128)(2,1)} async-done(((bf16[3,1,128,8192]{2,0,1,3:T(4,128)(2,1)}), bf16[3,1,128,8192]{2,0,1,3:T(4,128)(2,1)}, u32[]{:S(2)}, u32[]{:S(2)}) %all-to-all-start.4) | async-done | bytes 6291488 | tf_op jit(solution)/shard_map/all_to_all | solution.py:236
  1598.0 14.1 convert_bitcast_fusion
  1621.3 19.0 %fusion.80 = bf16[1,128,2048]{2,1,0:T(8,128)(2,1)} fusion(f32[128,2048]{1,0:T(8,128)S(1)} %copy-done.5, bf16[2048,8192]{1,0:T(8,128)(2,1)} %all-gather.17.cloned.1.call-done, f32[2,128,8192]{2,1,0:T(8,128)} %convolution_bitcast_fusion.2), kind=kOutput, calls=%fused_computation.106 | convolution fusion | flops 4301783040 | bytes 43515904 | tf_op jit(solution)/shard_map/tj,fj->tf/dot_general | solution.py:215
  1640.2 28.7 %all-to-all-done.3 = bf16[3,1,1024,256]{3,0,1,2:T(4,128)(2,1)S(1)} async-done(((bf16[3,1,1024,256]{3,0,1,2:T(4,128)(2,1)}), bf16[3,1,1024,256]{3,0,1,2:T(4,128)(2,1)S(1)}, u32[]{:S(2)}, u32[]{:S(2)}) %all-to-all-start.3) | async-done | bytes 1572896 | tf_op jit(solution)/shard_map/all_to_all | solution.py:293
  1673.8 13.6 fusion.107
  1687.4 38.0 %all-reduce.3 = (f32[2048]{0:T(1024)S(1)}, f32[2048]{0:T(1024)S(1)}) all-reduce(f32[2048]{0:T(1024)S(1)} %get-tuple-element.610, f32[2048]{0:T(1024)S(1)} %copy-done.22), channel_id=4, replica_groups=mesh['fsdp'=4,'seq'=8] {'fsdp','seq'}, use_global_device_ids=true, to_apply=%region_15.16.clone | all-reduce | flops 4096 | bytes 32768
  1737.1 77.2 %reduce-scatter.6.cloned.1.call-done = bf16[256,2,2048]{0,2,1:T(8,128)(2,1)} async-done(((bf16[1024,2,2048]{0,2,1:T(8,128)(2,1)}), bf16[256,2,2048]{0,2,1:T(8,128)(2,1)}) %reduce-scatter.6.cloned.1.call-update) | async-done | bytes 2097168 | tf_op jit(solution)/shard_map/reduce_scatter | solution.py:249
  (304 shorter events, 288.2 us)
Async XLA Ops:
  7.2 233.0 %all-gather.11.cloned.1.call-start = ((), (), s32[]{:S(2)}) async-start(), calls=%async_computation.8 | async-start | bytes 31457280 | tf_op jit(solution)/shard_map/all_gather | solution.py:192
  7.9 387.4 %all-gather.13.cloned.1.call-start = ((), (), s32[]{:S(2)}) async-start(), calls=%async_computation.9 | async-start | bytes 10485760 | tf_op jit(solution)/shard_map/all_gather | solution.py:193
  8.7 899.4 %all-gather.15.cloned.1.call-start = ((), (), s32[]{:S(2)}) async-start(), calls=%async_computation.10 | async-start | bytes 83886080 | tf_op jit(solution)/shard_map/all_gather | solution.py:210
  26.8 1180.0 %all-gather.17.cloned.1.call-start = ((), (), s32[]{:S(2)}) async-start(), calls=%async_computation.11 | async-start | bytes 41943040 | tf_op jit(solution)/shard_map/all_gather | solution.py:211
  27.5 347.3 %copy-start.20 = (f32[2048]{0:T(1024)}, f32[2048]{0:T(1024)S(1)}, u32[]{:S(2)}) copy-start(f32[2048]{0:T(1024)S(1)} %convert_element_type.204) | copy-start | bytes 24580
  28.7 346.2 %copy-start.23 = (f32[128]{0:T(128)}, f32[128]{0:T(128)S(1)}, u32[]{:S(2)}) copy-start(f32[128]{0:T(128)S(1)} %get-tuple-element.712) | copy-start | bytes 1540
  278.9 54.1 %all-to-all-start = ((bf16[3,1,128,2048]{2,0,1,3:T(4,128)(2,1)}), bf16[3,1,128,2048]{2,0,1,3:T(4,128)(2,1)S(1)}, u32[]{:S(2)}, u32[]{:S(2)}) async-start(bf16[3,1,128,2048]{2,0,1,3:T(4,128)(2,1)} %copy.196), calls=%async_computation | async-start | bytes 4194304 | tf_op jit(solution)/shard_map/all_to_all | solution.py:200
  370.7 19.5 %all-to-all-start.1 = ((bf16[8,2,16384]{2,1,0:T(2,128)(2,1)}), bf16[8,2,16384]{2,1,0:T(2,128)(2,1)}, u32[]{:S(2)}, u32[]{:S(2)}) async-start(bf16[8,2,16384]{2,1,0:T(2,128)(2,1)} %reshape.879), calls=%async_computation.1 | async-start | bytes 1048576 | tf_op jit(solution)/shard_map/all_to_all | solution.py:203
  374.8 1015.3 %all-gather.19.cloned.1.call-start = ((), (), s32[]{:S(2)}) async-start(), calls=%async_computation.12 | async-start | bytes 4718592 | tf_op jit(solution)/shard_map/all_gather | solution.py:271
  375.9 1029.6 %all-gather.23.cloned.1.call-start = ((), (), s32[]{:S(2)}) async-start(), calls=%async_computation.17 | async-start | bytes 4718592 | tf_op jit(solution)/shard_map/all_gather | solution.py:274
  401.8 849.5 %copy-start.4 = (f32[128,2048]{1,0:T(8,128)}, f32[128,2048]{1,0:T(8,128)S(1)}, u32[]{:S(2)}) copy-start(f32[128,2048]{1,0:T(8,128)S(1)} %get-tuple-element.716) | copy-start | bytes 3145732
  402.0 543.7 %copy-start.11 = (bf16[128,2048]{1,0:T(8,128)(2,1)}, bf16[128,2048]{1,0:T(8,128)(2,1)S(1)}, u32[]{:S(2)}) copy-start(bf16[128,2048]{1,0:T(8,128)(2,1)S(1)} %multiply_convert_fusion.2) | copy-start | bytes 1572868
  1252.9 324.7 %all-gather.21.cloned.1.call-start = ((), (), s32[]{:S(2)}) async-start(), calls=%async_computation.15 | async-start | bytes 4718592 | tf_op jit(solution)/shard_map/all_gather | solution.py:240
  1253.6 344.4 %all-gather.25.cloned.1.call-start = ((), (), s32[]{:S(2)}) async-start(), calls=%async_computation.18 | async-start | bytes 4718592 | tf_op jit(solution)/shard_map/all_gather | solution.py:237
  1278.4 32.9 %all-to-all-start.2 = ((bf16[8,2,16384]{2,1,0:T(2,128)(2,1)}), bf16[8,2,16384]{2,1,0:T(2,128)(2,1)S(1)}, u32[]{:S(2)}, u32[]{:S(2)}) async-start(bf16[8,2,16384]{2,1,0:T(2,128)(2,1)} %reshape.881), calls=%async_computation.2 | async-start | bytes 1048576 | tf_op jit(solution)/shard_map/all_to_all | solution.py:267
  1311.3 256.2 %all-to-all-start.4 = ((bf16[3,1,128,8192]{2,0,1,3:T(4,128)(2,1)}), bf16[3,1,128,8192]{2,0,1,3:T(4,128)(2,1)}, u32[]{:S(2)}, u32[]{:S(2)}) async-start(bf16[3,1,128,8192]{2,0,1,3:T(4,128)(2,1)} %copy.216), calls=%async_computation.5 | async-start | bytes 16777216 | tf_op jit(solution)/shard_map/all_to_all | solution.py:236
  1316.3 413.0 %all-reduce.6.cloned.1.call-start = ((), (), s32[]{:S(2)}) async-start(), calls=%async_computation.19 | async-start | bytes 8388608
  1405.5 327.3 %reduce-scatter.4.cloned.1.call-start = ((), (), s32[]{:S(2)}) async-start(), calls=%async_computation.13 | async-start | bytes 1310720 | tf_op jit(solution)/shard_map/reduce_scatter | solution.py:289
  1410.0 324.5 %reduce-scatter.8.cloned.1.call-start = ((), (), s32[]{:S(2)}) async-start(), calls=%async_computation.16 | async-start | bytes 5242880 | tf_op jit(solution)/shard_map/reduce_scatter | solution.py:252
  1587.1 227.2 %reduce-scatter.6.cloned.1.call-start = ((), (), s32[]{:S(2)}) async-start(), calls=%async_computation.14 | async-start | bytes 10485760 | tf_op jit(solution)/shard_map/reduce_scatter | solution.py:249
  1616.2 52.8 %all-to-all-start.3 = ((bf16[3,1,1024,256]{3,0,1,2:T(4,128)(2,1)}), bf16[3,1,1024,256]{3,0,1,2:T(4,128)(2,1)S(1)}, u32[]{:S(2)}, u32[]{:S(2)}) async-start(bf16[3,1,1024,256]{3,0,1,2:T(4,128)(2,1)} %copy.210), calls=%async_computation.3 | async-start | bytes 4194304 | tf_op jit(solution)/shard_map/all_to_all | solution.py:293
  1640.2 33.6 %copy-start.24 = (f32[128]{0:T(128)S(1)}, f32[128]{0:T(128)}, u32[]{:S(2)}) copy-start(f32[128]{0:T(128)} %copy-done.23) | copy-start | bytes 1540
  1673.8 52.8 %copy-start.12 = (f32[128,2048]{1,0:T(8,128)S(1)}, f32[128,2048]{1,0:T(8,128)}, u32[]{:S(2)}) copy-start(f32[128,2048]{1,0:T(8,128)} %get-tuple-element.683) | copy-start | bytes 3145732
  1673.8 52.8 %copy-start.27 = (f32[128]{0:T(128)S(1)}, f32[128]{0:T(128)}, u32[]{:S(2)}) copy-start(f32[128]{0:T(128)} %get-tuple-element.711) | copy-start | bytes 1540
  (27 other events, 245.6 us)
Sparse Core Ops, SparseCore 0:
  9.8 230.2 all-gather.10
  242.0 87.4 all-gather.12
  331.4 576.6 all-gather.14
  909.8 297.0 all-gather.16
  1208.3 46.8 all-gather.18
  1257.3 56.8 all-gather.22
  1315.8 78.7 all-gather.20
  1396.2 135.9 all-gather.24
  1536.0 101.4 all-reduce.5
  1640.3 27.9 reduce-scatter.3
  1671.2 53.6 reduce-scatter.7
  1727.8 86.4 reduce-scatter.5
where the time goes:
time: 1840 us; the launch traced here: 1830 us
  waiting for transfers between devices  1320 us (72%)
  matrix products  220 us (12%)
  local copies, waits for them, and re-layouts  140 us (8%)
  other arithmetic  72.3 us (4%)
  blocking collectives  38 us (2%)
  starting transfers between devices  23.7 us (1%)
    all_gather x1, waiting for transfers between devices, body(): lax.all_gather(w_gate_up, 'fsdp', axis=0, tiled=True)  506 us
    all_gather x1, waiting for transfers between devices, body(): lax.all_gather(w_down, 'fsdp', axis=0, tiled=True)  261 us
    all_gather x1, waiting for transfers between devices, body(): lax.all_gather(w_qkv, 'fsdp', axis=0, tiled=True)  211 us
    all_to_all x1, waiting for transfers between devices, body(): lax.all_to_all(unit_rows, 'seq', split_axis=3, concat_axis=2, tiled=True)  157 us
    reduce_scatter x1, waiting for transfers between devices, body(): lax.psum_scatter(gu_part.astype(jnp.bfloat16), 'fsdp', scatter_dimension=...  77.2 us
    all_to_all x1, waiting for transfers between devices, body(): lax.all_to_all(stacked, 'seq', split_axis=3, concat_axis=2, tiled=True)  49 us
    unnamed x69, local copies, waits for them, and re-layouts  43.5 us
    unnamed x1, blocking collectives  38 us
  transfers between devices with their start and end apart: 17, of which 9 were waited for; matrix products, arithmetic and copies ran while one was open for 23% of the time, Pallas kernels for 0%

commit v1 on v0

--- a/solution.py
+++ b/solution.py
@@ -178,6 +178,13 @@
 
 
 def body(residual_in, attn_gain, mlp_gain, w_qkv, w_out, w_gate_up, w_down, cotangent):
+
+    def measure_threads(mat, along_dim, at_axis):
+        newest = jnp.split(mat, lax.axis_size("seq"), axis=along_dim)
+        aux = jnp.stack(newest, axis=0)
+        part_next = jnp.concatenate(lax.all_to_all(aux, "seq", 0, 0), axis=at_axis)
+        return part_next
+
     seq_count, shard_len, model_width = residual_in.shape
     tokens = seq_count * shard_len
     seq_index = lax.axis_index("seq")
@@ -197,7 +204,7 @@
     key_rows = (projected[1] * cosine + rotate(projected[1]) * sine_table).astype(jnp.bfloat16)
     values = projected[2].astype(jnp.bfloat16)
     stacked = jnp.stack([queries, key_rows, values]).reshape(3, seq_count, shard_len, model_width)
-    head_view = lax.all_to_all(stacked, "seq", split_axis=3, concat_axis=2, tiled=True)
+    head_view = measure_threads(stacked, 3, 2)
     attended, totals = attend_forward(head_view[0], head_view[1], head_view[2])
     attended_heads = attended.astype(jnp.bfloat16)
     sent_back = lax.all_to_all(attended_heads, "seq", split_axis=1, concat_axis=2, tiled=True)

time: 1840 us -> 1840 us (level)
    unnamed x69 -> x74, local copies, waits for them, and re-layouts: 43.5 us -> 49.3 us
where the time goes in v1:
time: 1840 us; the launch traced here: 1830 us
  waiting for transfers between devices  1320 us (72%)
  matrix products  220 us (12%)
  local copies, waits for them, and re-layouts  139 us (8%)
  other arithmetic  72.3 us (4%)
  blocking collectives  38 us (2%)
  starting transfers between devices  23.7 us (1%)
    all_gather x1, waiting for transfers between devices, body(): lax.all_gather(w_gate_up, 'fsdp', axis=0, tiled=True)  520 us
    all_gather x1, waiting for transfers between devices, body(): lax.all_gather(w_down, 'fsdp', axis=0, tiled=True)  261 us
    all_gather x1, waiting for transfers between devices, body(): lax.all_gather(w_qkv, 'fsdp', axis=0, tiled=True)  211 us
    all_to_all x1, waiting for transfers between devices, body(): lax.all_to_all(unit_rows, 'seq', split_axis=3, concat_axis=2, tiled=True)  156 us
    reduce_scatter x1, waiting for transfers between devices, body(): lax.psum_scatter(gu_part.astype(jnp.bfloat16), 'fsdp', scatter_dimension=...  77.3 us
    unnamed x74, local copies, waits for them, and re-layouts  49.3 us
    unnamed x1, blocking collectives  38 us
    all_to_all x1, waiting for transfers between devices, measure_threads(): part_next = jnp.concatenate(lax.all_to_all(aux, 'seq', 0, 0), axis=at_axis)  37.8 us
  transfers between devices with their start and end apart: 17, of which 9 were waited for; matrix products, arithmetic and copies ran while one was open for 23% of the time, Pallas kernels for 0%

profile of v1, /device:TPU:0, one launch (start us, length us, event | category | flops | bytes accessed | tf_op | source)
XLA Modules:
  0.0 1827.8 jit_solution(17514729585084769290)
XLA Ops:
  8.7 18.1 copy.202
  28.7 211.5 %all-gather.11.cloned.1.call-done = bf16[2048,3,2048]{2,0,1:T(8,128)(2,1)} async-done(((bf16[512,3,2048]{2,0,1:T(8,128)(2,1)}), bf16[2048,3,2048]{2,0,1:T(8,128)(2,1)}) %all-gather.11.cloned.1.call-update) | async-done | bytes 25165840 | tf_op jit(solution)/shard_map/all_gather | solution.py:199
  240.2 13.5 convolution_bitcast_fusion.3
  286.9 37.8 %all-to-all-done = bf16[8,3,1,128,256]{4,3,1,2,0:T(8,128)(2,1)S(1)} async-done(((bf16[8,3,1,128,256]{4,3,1,2,0:T(8,128)(2,1)}), bf16[8,3,1,128,256]{4,3,1,2,0:T(8,128)(2,1)S(1)}, u32[]{:S(2)}, u32[]{:S(2)}) %all-to-all-start) | async-done | bytes 1572896 | tf_op jit(solution)/shard_map/all_to_all | solution.py:185
  326.6 16.6 while.118
  333.3 9.9 while.121
  362.3 13.7 all-to-all-done.1
  387.8 520.3 %all-gather.15.cloned.1.call-done = bf16[8192,2,2048]{2,0,1:T(8,128)(2,1)} async-done(((bf16[2048,2,2048]{2,0,1:T(8,128)(2,1)}), bf16[8192,2,2048]{2,0,1:T(8,128)(2,1)}) %all-gather.15.cloned.1.call-update) | async-done | bytes 67108880 | tf_op jit(solution)/shard_map/all_gather | solution.py:217
  908.1 37.6 %convolution_bitcast_fusion.2 = f32[2,128,8192]{2,1,0:T(8,128)} fusion(bf16[8192,2,2048]{2,0,1:T(8,128)(2,1)} %all-gather.15.cloned.1.call-done, bf16[128,2048]{1,0:T(8,128)(2,1)S(1)} %multiply_convert_fusion.2), kind=kOutput, calls=%fused_computation.67 | convolution fusion | flops 8589934592 | bytes 76021760 | tf_op jit(solution)/shard_map/td,jpd->ptj/dot_general | solution.py:220
  945.7 261.2 %all-gather.17.cloned.1.call-done = bf16[2048,8192]{1,0:T(8,128)(2,1)} async-done(((bf16[512,8192]{1,0:T(8,128)(2,1)}), bf16[2048,8192]{1,0:T(8,128)(2,1)}) %all-gather.17.cloned.1.call-update) | async-done | bytes 33554448 | tf_op jit(solution)/shard_map/all_gather | solution.py:218
  1206.9 19.1 %fusion.83 = (bf16[1,128,8192]{2,1,0:T(8,128)(2,1)}, bf16[1,128,8192]{2,1,0:T(8,128)(2,1)}) fusion(f32[2,128,8192]{2,1,0:T(8,128)} %convolution_bitcast_fusion.2, bf16[2048,8192]{1,0:T(8,128)(2,1)} %all-gather.17.cloned.1.call-done, bf16[1,128,2048]{2,1,0:T(8,128)(2,1)} %param.23), kind=kOutput, calls=%fused_computation.108 | convolution fusion | flops 4308598784 | bytes 46661632 | tf_op jit(solution)/shard_map/tf,fj->tj/dot_general | solution.py:231
  1226.0 25.4 %multiply_reduce_fusion = (f32[2048]{0:T(1024)}, f32[128]{0:T(128)S(1)}, f32[128,2048]{1,0:T(8,128)S(1)}) fusion(f32[128,2048]{1,0:T(8,128)S(1)} %get-tuple-element.731, f32[128]{0:T(128)S(1)} %get-tuple-element.729, f32[2048]{0:T(1024)S(1)} %convert_element_type.212, bf16[8192,2,2048]{2,0,1:T(8,128)(2,1)} %all-gather.15.cloned.1.call-done, ...), kind=kOutput, calls=%fused_computation.151 | convolution fusion | flops 8593602560 | bytes 73417728 | tf_op jit(solution)/shard_map/ptj,jpd->td/dot_general | solution.py:236
  1266.0 11.5 reduce.4
  1289.4 13.2 copy.216
  1329.2 37.6 %while.120 = (s32[]{:T(128)}, f32[1,1024,4,64]{1,3,2,0:T(8,128)}, f32[1,1024,4,64]{1,3,2,0:T(8,128)S(1)}, f32[1,1024,4,64]{1,3,2,0:T(8,128)}, bf16[1,1024,4,64]{...) while((s32[]{:T(128)}, f32[1,1024,4,64]{1,3,2,0:T(8,128)}, ...), condition=%wide.region_12.13_spmd, body=%wide.region_9.12_spmd.sunk | while | flops 340329248 | bytes 17070880 | solution.py:170
  1331.0 10.8 while.122
  1344.4 21.6 %while.122 = (s32[]{:T(128)}, f32[1,512,4,64]{1,3,2,0:T(8,128)S(1)}, f32[1,1024,4,64]{1,3,2,0:T(8,128)S(1)}, f32[1,1024,4,64]{1,3,2,0:T(8,128)}, s32[]{:T(128)},...) while((s32[]{:T(128)}, f32[1,512,4,64]{1,3,2,0:T(8,128)S(1)}, ...), condition=%wide.region_11.11_spmd.clone, body=%wide.region_10.10_spmd.clone.sunk | while | flops 340329216 | bytes 14432507 | solution.py:163
  1411.4 156.1 %all-to-all-done.4 = bf16[3,1,128,8192]{2,0,1,3:T(4,128)(2,1)} async-done(((bf16[3,1,128,8192]{2,0,1,3:T(4,128)(2,1)}), bf16[3,1,128,8192]{2,0,1,3:T(4,128)(2,1)}, u32[]{:S(2)}, u32[]{:S(2)}) %all-to-all-start.4) | async-done | bytes 6291488 | tf_op jit(solution)/shard_map/all_to_all | solution.py:243
  1598.0 14.1 convert_bitcast_fusion
  1621.2 19.0 %fusion.80 = bf16[1,128,2048]{2,1,0:T(8,128)(2,1)} fusion(f32[128,2048]{1,0:T(8,128)S(1)} %copy-done.5, bf16[2048,8192]{1,0:T(8,128)(2,1)} %all-gather.17.cloned.1.call-done, f32[2,128,8192]{2,1,0:T(8,128)} %convolution_bitcast_fusion.2), kind=kOutput, calls=%fused_computation.106 | convolution fusion | flops 4301783040 | bytes 43515904 | tf_op jit(solution)/shard_map/tj,fj->tf/dot_general | solution.py:222
  1640.2 28.7 %all-to-all-done.3 = bf16[3,1,1024,256]{3,0,1,2:T(4,128)(2,1)S(1)} async-done(((bf16[3,1,1024,256]{3,0,1,2:T(4,128)(2,1)}), bf16[3,1,1024,256]{3,0,1,2:T(4,128)(2,1)S(1)}, u32[]{:S(2)}, u32[]{:S(2)}) %all-to-all-start.3) | async-done | bytes 1572896 | tf_op jit(solution)/shard_map/all_to_all | solution.py:300
  1673.8 13.6 fusion.107
  1687.4 38.0 %all-reduce.3 = (f32[2048]{0:T(1024)S(1)}, f32[2048]{0:T(1024)S(1)}) all-reduce(f32[2048]{0:T(1024)S(1)} %get-tuple-element.625, f32[2048]{0:T(1024)S(1)} %copy-done.21), channel_id=4, replica_groups=mesh['fsdp'=4,'seq'=8] {'fsdp','seq'}, use_global_device_ids=true, to_apply=%region_15.16.clone | all-reduce | flops 4096 | bytes 32768
  1737.1 77.3 %reduce-scatter.6.cloned.1.call-done = bf16[256,2,2048]{0,2,1:T(8,128)(2,1)} async-done(((bf16[1024,2,2048]{0,2,1:T(8,128)(2,1)}), bf16[256,2,2048]{0,2,1:T(8,128)(2,1)}) %reduce-scatter.6.cloned.1.call-update) | async-done | bytes 2097168 | tf_op jit(solution)/shard_map/reduce_scatter | solution.py:256
  (309 shorter events, 286.6 us)
Async XLA Ops:
  7.2 233.0 %all-gather.11.cloned.1.call-start = ((), (), s32[]{:S(2)}) async-start(), calls=%async_computation.8 | async-start | bytes 31457280 | tf_op jit(solution)/shard_map/all_gather | solution.py:199
  7.9 373.2 %all-gather.13.cloned.1.call-start = ((), (), s32[]{:S(2)}) async-start(), calls=%async_computation.9 | async-start | bytes 10485760 | tf_op jit(solution)/shard_map/all_gather | solution.py:200
  8.7 899.4 %all-gather.15.cloned.1.call-start = ((), (), s32[]{:S(2)}) async-start(), calls=%async_computation.10 | async-start | bytes 83886080 | tf_op jit(solution)/shard_map/all_gather | solution.py:217
  26.9 1180.0 %all-gather.17.cloned.1.call-start = ((), (), s32[]{:S(2)}) async-start(), calls=%async_computation.11 | async-start | bytes 41943040 | tf_op jit(solution)/shard_map/all_gather | solution.py:218
  27.5 333.1 %copy-start.19 = (f32[2048]{0:T(1024)}, f32[2048]{0:T(1024)S(1)}, u32[]{:S(2)}) copy-start(f32[2048]{0:T(1024)S(1)} %convert_element_type.204) | copy-start | bytes 24580
  28.7 332.0 %copy-start.22 = (f32[128]{0:T(128)}, f32[128]{0:T(128)S(1)}, u32[]{:S(2)}) copy-start(f32[128]{0:T(128)S(1)} %get-tuple-element.727) | copy-start | bytes 1540
  282.0 42.7 %all-to-all-start = ((bf16[8,3,1,128,256]{4,3,1,2,0:T(8,128)(2,1)}), bf16[8,3,1,128,256]{4,3,1,2,0:T(8,128)(2,1)S(1)}, u32[]{:S(2)}, u32[]{:S(2)}) async-start(bf16[8,3,1,128,256]{4,3,1,2,0:T(8,128)(2,1)} %fusion.123), calls=%async_computation | async-start | bytes 3145728 | tf_op jit(solution)/shard_map/all_to_all | solution.py:185
  356.4 19.5 %all-to-all-start.1 = ((bf16[8,2,16384]{2,1,0:T(2,128)(2,1)}), bf16[8,2,16384]{2,1,0:T(2,128)(2,1)}, u32[]{:S(2)}, u32[]{:S(2)}) async-start(bf16[8,2,16384]{2,1,0:T(2,128)(2,1)} %reshape.884), calls=%async_computation.1 | async-start | bytes 1048576 | tf_op jit(solution)/shard_map/all_to_all | solution.py:210
  360.6 1029.7 %all-gather.19.cloned.1.call-start = ((), (), s32[]{:S(2)}) async-start(), calls=%async_computation.12 | async-start | bytes 4718592 | tf_op jit(solution)/shard_map/all_gather | solution.py:278
  361.7 1044.3 %all-gather.23.cloned.1.call-start = ((), (), s32[]{:S(2)}) async-start(), calls=%async_computation.17 | async-start | bytes 4718592 | tf_op jit(solution)/shard_map/all_gather | solution.py:281
  387.6 863.7 %copy-start.4 = (f32[128,2048]{1,0:T(8,128)}, f32[128,2048]{1,0:T(8,128)S(1)}, u32[]{:S(2)}) copy-start(f32[128,2048]{1,0:T(8,128)S(1)} %get-tuple-element.731) | copy-start | bytes 3145732
  387.8 557.9 %copy-start.11 = (bf16[128,2048]{1,0:T(8,128)(2,1)}, bf16[128,2048]{1,0:T(8,128)(2,1)S(1)}, u32[]{:S(2)}) copy-start(bf16[128,2048]{1,0:T(8,128)(2,1)S(1)} %multiply_convert_fusion.2) | copy-start | bytes 1572868
  1226.0 25.4 %copy-start.15 = (bf16[1,128,2048]{2,1,0:T(8,128)(2,1)S(1)}, bf16[1,128,2048]{2,1,0:T(8,128)(2,1)}, u32[]{:S(2)}) copy-start(bf16[1,128,2048]{2,1,0:T(8,128)(2,1)} %param.23) | copy-start | bytes 1572868
  1252.9 324.7 %all-gather.21.cloned.1.call-start = ((), (), s32[]{:S(2)}) async-start(), calls=%async_computation.15 | async-start | bytes 4718592 | tf_op jit(solution)/shard_map/all_gather | solution.py:247
  1253.6 344.4 %all-gather.25.cloned.1.call-start = ((), (), s32[]{:S(2)}) async-start(), calls=%async_computation.18 | async-start | bytes 4718592 | tf_op jit(solution)/shard_map/all_gather | solution.py:244
  1278.5 32.9 %all-to-all-start.2 = ((bf16[8,2,16384]{2,1,0:T(2,128)(2,1)}), bf16[8,2,16384]{2,1,0:T(2,128)(2,1)S(1)}, u32[]{:S(2)}, u32[]{:S(2)}) async-start(bf16[8,2,16384]{2,1,0:T(2,128)(2,1)} %reshape.886), calls=%async_computation.2 | async-start | bytes 1048576 | tf_op jit(solution)/shard_map/all_to_all | solution.py:274
  1311.3 256.2 %all-to-all-start.4 = ((bf16[3,1,128,8192]{2,0,1,3:T(4,128)(2,1)}), bf16[3,1,128,8192]{2,0,1,3:T(4,128)(2,1)}, u32[]{:S(2)}, u32[]{:S(2)}) async-start(bf16[3,1,128,8192]{2,0,1,3:T(4,128)(2,1)} %copy.216), calls=%async_computation.5 | async-start | bytes 16777216 | tf_op jit(solution)/shard_map/all_to_all | solution.py:243
  1316.3 412.9 %all-reduce.6.cloned.1.call-start = ((), (), s32[]{:S(2)}) async-start(), calls=%async_computation.19 | async-start | bytes 8388608
  1405.9 326.7 %reduce-scatter.4.cloned.1.call-start = ((), (), s32[]{:S(2)}) async-start(), calls=%async_computation.13 | async-start | bytes 1310720 | tf_op jit(solution)/shard_map/reduce_scatter | solution.py:296
  1411.4 323.1 %reduce-scatter.8.cloned.1.call-start = ((), (), s32[]{:S(2)}) async-start(), calls=%async_computation.16 | async-start | bytes 5242880 | tf_op jit(solution)/shard_map/reduce_scatter | solution.py:259
  1587.1 227.3 %reduce-scatter.6.cloned.1.call-start = ((), (), s32[]{:S(2)}) async-start(), calls=%async_computation.14 | async-start | bytes 10485760 | tf_op jit(solution)/shard_map/reduce_scatter | solution.py:256
  1616.1 52.7 %all-to-all-start.3 = ((bf16[3,1,1024,256]{3,0,1,2:T(4,128)(2,1)}), bf16[3,1,1024,256]{3,0,1,2:T(4,128)(2,1)S(1)}, u32[]{:S(2)}, u32[]{:S(2)}) async-start(bf16[3,1,1024,256]{3,0,1,2:T(4,128)(2,1)} %copy.210), calls=%async_computation.3 | async-start | bytes 4194304 | tf_op jit(solution)/shard_map/all_to_all | solution.py:300
  1673.8 52.7 %copy-start.12 = (f32[128,2048]{1,0:T(8,128)S(1)}, f32[128,2048]{1,0:T(8,128)}, u32[]{:S(2)}) copy-start(f32[128,2048]{1,0:T(8,128)} %get-tuple-element.698) | copy-start | bytes 3145732
  1673.8 52.7 %copy-start.26 = (f32[128]{0:T(128)S(1)}, f32[128]{0:T(128)}, u32[]{:S(2)}) copy-start(f32[128]{0:T(128)} %get-tuple-element.726) | copy-start | bytes 1540
  (26 other events, 145.5 us)
Sparse Core Ops, SparseCore 0:
  9.8 230.2 all-gather.10
  242.0 87.4 all-gather.12
  331.4 576.6 all-gather.14
  909.8 297.0 all-gather.16
  1208.3 46.8 all-gather.18
  1257.3 56.8 all-gather.22
  1315.8 78.7 all-gather.20
  1396.2 135.9 all-gather.24
  1536.1 101.4 all-reduce.5
  1640.3 27.9 reduce-scatter.3
  1671.2 53.6 reduce-scatter.7
  1727.9 86.4 reduce-scatter.5
